TPU v7x, 32 devices: a whole 2x2x4 slice. The times are simulated.
32 devices in a mesh: groups: 2 (over x), ctx: 16 (over z, y, core).
Axes of the slice: x: 2, y: 2, z: 4, core: 2. Of those that a mesh axis runs over, the one named last changes fastest.
Arguments:
- query_latent: bfloat16 [96, 8192], P(('groups', 'ctx')), parts along dimension 0, may hold values from -512 to 512
- query_rope: bfloat16 [96, 1024], P(('groups', 'ctx')), parts along dimension 0, may hold values from -18 to 18
- cache_latent: bfloat16 [16384, 512], P(('groups', 'ctx')), parts along dimension 0, may hold values from -4 to 4
- cache_rope: bfloat16 [128, 8192], P('groups', 'ctx'), parts along dimension 0, may hold values from -4 to 4
- valid_len: int32 [96], P('groups'), parts along dimension 0, may hold values from 2048 to 8192
- w_vo: bfloat16 [8192, 2560], P('ctx'), may hold values from -0.29882812 to 0.29882812
- residual: bfloat16 [96, 2560], P(('groups', 'ctx')), parts along dimension 0, may hold values from -6 to 6
- norm_gain: float32 [2560], replicated, may hold values from 0.25 to 1.75
- expert_ids: int32 [96, 6], P('groups'), parts along dimension 0, may hold values from 0 to 15, all different within a row; in each aligned block of 48 rows (0 to 47, 48 to 95, ...) at most 36 rows name the same one
- route_weight: float32 [96, 6], P('groups'), parts along dimension 0, may hold values from 0.1 to 0.4
- w_gate: bfloat16 [16, 2560, 768], P('ctx'), may hold values from -0.125 to 0.125
- w_up: bfloat16 [16, 2560, 768], P('ctx'), may hold values from -0.125 to 0.125
- w_down: bfloat16 [16, 768, 2560], P('ctx'), may hold values from -0.21875 to 0.21875
Outputs:
- attn_out: bfloat16 [96, 2560], P(('groups', 'ctx')), parts along dimension 0
- layer_out: bfloat16 [96, 2560], P(('groups', 'ctx')), parts along dimension 0
There are 2 independent parts, one for each index of `groups`. A program takes and returns all parts, laid end to end along the dimension named above; an argument that names none is the same for every part. Nothing has to cross between parts.
Inputs may be any that keep to these rules, and one draw needn't show every extreme that they name: `expert_ids`: each row names 6 different experts; no expert is named by more than 36 rows, a bound that some block reaches.
All inputs are finite; a program needn't handle non-finite values.
Results may differ from a plain program's by a relative error of at most 0.006.
Values may be sent and summed in bfloat16 or wider, within the bound.
No kernel may reach another device: no remote copies, remote signals or barrier semaphores. Data moves between devices by JAX's collectives and lax.ppermute only.
A program may use at most 128 MiB of HBM per device.

v0:
```python
import functools
import math

import jax
import jax.numpy as jnp
import numpy as np
from jax import lax
from jax.experimental import pallas as pl
from jax.experimental.pallas import tpu as pltpu
from jax.sharding import PartitionSpec as P


softmax_scale = 192.0 ** (-0.5)
negative_fill = -1e30
norm_eps = 1e-06
exponent_scale = softmax_scale * math.log2(math.e)
no_position = -1e29
share = 4
strip = 512

VMEM = pltpu.VMEM
SMEM = pltpu.SMEM
f32 = jnp.float32
bf16 = jnp.bfloat16


def expert_apply(inputs, gate_weight, up_weight, down_weight):
    gate_out = jnp.dot(inputs, gate_weight, preferred_element_type=jnp.float32)
    up_out = jnp.dot(inputs, up_weight, preferred_element_type=jnp.float32)
    hidden = (jax.nn.silu(gate_out) * up_out).astype(jnp.bfloat16)
    return jnp.dot(hidden, down_weight, preferred_element_type=jnp.float32).astype(jnp.bfloat16)


def plain_layer(
    query_latent,
    query_rope,
    cache_latent,
    cache_rope,
    valid_len,
    w_vo,
    residual,
    norm_gain,
    expert_ids,
    route_weight,
    w_gate,
    w_up,
    w_down,
):
    query_all, rope_all = (
        lax.all_gather(query_latent, "ctx", axis=0, tiled=True),
        lax.all_gather(query_rope, "ctx", axis=0, tiled=True),
    )
    total_rows = query_all.shape[0]
    own_rows = residual.shape[0]
    latent = cache_latent.shape[1]
    rope_dim = cache_rope.shape[0]
    head_count = rope_all.shape[1] // rope_dim
    block_len = cache_latent.shape[0]
    devices = lax.axis_size("ctx")
    self_index = lax.axis_index("ctx")
    col_count = head_count * latent // devices
    flat_query = query_all.reshape(total_rows * head_count, latent)
    flat_rope = rope_all.reshape(total_rows * head_count, rope_dim)
    scores = lax.dot_general(
        flat_query, cache_latent, (((1,), (1,)), ((), ())), preferred_element_type=jnp.float32
    )
    scores = (
        scores + jnp.dot(flat_rope, cache_rope, preferred_element_type=jnp.float32)
    ) * softmax_scale
    position = self_index * block_len + lax.broadcasted_iota(jnp.int32, (1, block_len), 1)
    usable = position < jnp.repeat(valid_len, head_count)[:, None]
    block_max = jnp.max(jnp.where(usable, scores, negative_fill), axis=1)
    weights = jnp.where(usable, jnp.exp(scores - block_max[:, None]), 0.0).astype(jnp.bfloat16)
    block_sum = jnp.sum(weights.astype(jnp.float32), axis=1)
    block_out = jnp.dot(weights, cache_latent, preferred_element_type=jnp.float32)
    row_max = block_max.reshape(total_rows, head_count)
    row_sum = block_sum.reshape(total_rows, head_count)
    global_max = lax.pmax(row_max, "ctx")
    factor = jnp.exp(row_max - global_max)
    scaled = (block_out.reshape(total_rows, head_count, latent) * factor[:, :, None]).reshape(
        total_rows, head_count * latent
    )
    merged = lax.psum_scatter(scaled, "ctx", scatter_dimension=1, tiled=True)
    totals = lax.psum(row_sum * factor, "ctx")
    divisor = lax.dynamic_slice_in_dim(totals, self_index * col_count // latent, 1, 1)
    attention = (merged / divisor).astype(jnp.bfloat16)
    projected = lax.psum_scatter(
        jnp.dot(attention, w_vo, preferred_element_type=jnp.float32),
        "ctx",
        scatter_dimension=0,
        tiled=True,
    )
    hidden_state = residual.astype(jnp.float32) + projected
    normed = (
        hidden_state
        * lax.rsqrt(jnp.mean(hidden_state * hidden_state, axis=1, keepdims=True) + norm_eps)
        * norm_gain
    ).astype(jnp.bfloat16)
    expert_iota = lax.broadcasted_iota(jnp.int32, (1, 1, devices), 2)
    route_table = jnp.sum(
        jnp.where(expert_ids[:, :, None] == expert_iota, route_weight[:, :, None], 0.0), axis=1
    )
    gate_own = w_gate[0]
    up_own = w_up[0]
    down_own = w_down[0]
    own_table = jnp.transpose(
        lax.dynamic_slice_in_dim(route_table, self_index * own_rows, own_rows, 0)
    )
    outgoing = jnp.where(
        own_table[:, :, None] > 0.0, normed[None, :, :], jnp.zeros((), jnp.bfloat16)
    )
    arrived = lax.all_to_all(outgoing, "ctx", split_axis=0, concat_axis=0, tiled=True)
    item_count = arrived.shape[1]
    stacked = arrived.reshape(devices * item_count, arrived.shape[2])
    result = expert_apply(stacked, gate_own, up_own, down_own).reshape(
        devices, item_count, arrived.shape[2]
    )
    returned = lax.all_to_all(result, "ctx", split_axis=0, concat_axis=0, tiled=True)
    mixture = jnp.sum(own_table[:, :, None] * returned.astype(jnp.float32), axis=0)
    layer_out = (hidden_state + mixture).astype(jnp.bfloat16)
    return (projected.astype(jnp.bfloat16), layer_out)


def place(device):
    return 2 * ((device // 2 ^ device // 4) & 1) + device % 2


def call(kernel, out_shape, *operands, spaces=None, scratch=(), limit=24, out_space=VMEM):
    spaces = spaces or {}
    in_specs = [pl.BlockSpec(memory_space=spaces.get(i, VMEM)) for i in range(len(operands))]
    many = isinstance(out_shape, (tuple, list))
    out_specs = [pl.BlockSpec(memory_space=VMEM) for _ in out_shape] if many else pl.BlockSpec(memory_space=out_space)
    return pl.pallas_call(
        kernel,
        out_shape=out_shape,
        in_specs=in_specs,
        out_specs=out_specs,
        scratch_shapes=list(scratch),
        compiler_params=pltpu.CompilerParams(vmem_limit_bytes=limit << 20),
        cost_estimate=pl.CostEstimate(flops=4 * 10**9, bytes_accessed=64 << 20, transcendentals=0),
    )(*operands)


def strip_order(rows, devices, strips, height):
    order = np.zeros((devices * height, strips * rows * devices), np.float32)
    for device in range(devices):
        for row in range(rows):
            for part in range(strips):
                order[device * height + row * strips + part, part * rows * devices + device * rows + row] = 1.0
    return order


def prepare(heads_each, query_hbm, rope_hbm, out_hbm, query_ref, rope_ref, piece, rope_piece, packed, arrive, leave):
    fetches = [
        pltpu.make_async_copy(query_hbm, query_ref, arrive.at[0]),
        pltpu.make_async_copy(rope_hbm, rope_ref, arrive.at[1]),
    ]
    for fetch in fetches:
        fetch.start()
    rows = query_ref.shape[0]
    per = rows * heads_each
    latent = query_ref.shape[1] // (heads_each * share)
    rope_dim = rope_ref.shape[1] // (heads_each * share)
    half_width = latent // 2
    devices = out_hbm.shape[0]
    lane = lax.broadcasted_iota(jnp.int32, (8, 128), 1)
    rope_piece[...] = jnp.zeros_like(rope_piece)
    for fetch in fetches:
        fetch.wait()
    query = query_ref[...].astype(f32)
    rope = rope_ref[...].astype(f32)
    sends = []
    for kind in range(share):
        owners = [device for device in range(devices) if place(device) == kind]
        for item in range(per):
            row, index = divmod(item, heads_each)
            head = owners[index]
            for half in range(2):
                begin = head * latent + half * half_width
                piece[kind, half * per + item : half * per + item + 1, :] = query[row : row + 1, begin : begin + half_width]
            block = head * rope_dim // 128
            rope_piece[kind, item : item + 1, :] = rope[row : row + 1, block * 128 : (block + 1) * 128]
        first = rope_piece[kind, 0:8, :]
        second = rope_piece[kind, 8:16, :]
        if kind % 2 == 1:
            first = pltpu.roll(first, 64, 1)
        else:
            second = pltpu.roll(second, 64, 1)
        row_tiles, lane_tiles = 2 * per // 8, half_width // 128
        for rt in range(row_tiles):
            for lt in range(lane_tiles):
                tile = piece[kind, rt * 8 : (rt + 1) * 8, lt * 128 : (lt + 1) * 128]
                packed[kind, rt * lane_tiles + lt] = tile.astype(bf16)
        packed[kind, row_tiles * lane_tiles] = jnp.where(lane < 64, first, second).astype(bf16)
        for device in owners:
            send = pltpu.make_async_copy(packed.at[kind], out_hbm.at[device], leave.at[device])
            send.start()
            sends.append(send)
    for send in sends:
        send.wait()


def place_of(item, source, rows, heads_each, total_rows):
    row = sum((item >= step * heads_each).astype(jnp.int32) for step in range(1, rows))
    head = item - row * heads_each
    core, chip = lax.rem(source, 2), lax.shift_right_logical(source, 1)
    return head * total_rows + core * (total_rows // 2) + chip * rows + row


def one_hot(target, height):
    return (lax.broadcasted_iota(jnp.int32, (height, target.shape[1]), 0) == target).astype(f32).astype(bf16)


def tables(rows, heads_each, length_ref, order_ref, rope_order_ref, limit_ref):
    total_rows = limit_ref.shape[0]
    devices = total_rows // rows
    flat = heads_each * total_rows
    per = rows * heads_each
    for row in range(total_rows):
        device, index = divmod(row, rows)
        at = device % 2 * (total_rows // 2) + device // 2 * rows + index
        limit_ref[at : at + 1, :] = jnp.full((1, 128), length_ref[row], jnp.int32)
    column = lax.broadcasted_iota(jnp.int32, (1, order_ref.shape[1]), 1)
    source = lax.rem(lax.shift_right_logical(column, 3), devices)
    unit = lax.div(column, devices * 8) * 8 + lax.rem(column, 8)
    second = (unit >= per).astype(jnp.int32)
    target = second * flat + place_of(unit - second * per, source, rows, heads_each, total_rows)
    order_ref[...] = one_hot(target, 2 * flat)
    column = lax.broadcasted_iota(jnp.int32, (1, devices * 8), 1)
    source = lax.shift_right_logical(column, 3)
    item = lax.rem(column, 8)
    for half in range(2):
        shifted = item + 8 * half
        target = jnp.where(shifted < per, place_of(shifted, source, rows, heads_each, total_rows), -1)
        rope_order_ref[half * flat : (half + 1) * flat, :] = one_hot(target, flat)


def score_block(query, rope_query, keys, rope_keys, begin, limits, heads_each):
    flat, _ = query.shape
    total_rows = flat // heads_each
    block_len = rope_keys.shape[1]
    empty = jnp.zeros_like(rope_keys)
    rope_keys = jnp.concatenate([rope_keys, empty, empty, rope_keys], axis=0)
    scores = lax.dot_general(query, keys, (((1,), (1,)), ((), ())), preferred_element_type=f32)
    scores = scores + jnp.dot(rope_query, rope_keys, preferred_element_type=f32)
    valid = lax.broadcasted_iota(jnp.int32, (total_rows, block_len), 1) + begin < limits
    return jnp.where(valid[None], scores.reshape(heads_each, total_rows, block_len), negative_fill).reshape(flat, block_len)


def score_near(heads_each, arrived_ref, order_ref, rope_order_ref, limit_ref, own_ref, own_rope_ref, core_ref, core_rope_ref, query_ref, rope_query_ref, scores_ref):
    devices = arrived_ref.shape[0]
    flat = order_ref.shape[0] // 2
    row_tiles = arrived_ref.shape[1] // 2
    block_len, _ = own_ref.shape
    me = lax.axis_index("ctx")
    gathered = jnp.concatenate(
        [
            jnp.concatenate(
                [arrived_ref[:, 2 * rt + lt].reshape(devices * 8, 128) for lt in range(2)], axis=1
            )
            for rt in range(row_tiles)
        ],
        axis=0,
    )
    ordered = jnp.dot(order_ref[...], gathered, preferred_element_type=f32).astype(bf16)
    query = jnp.concatenate([ordered[:flat], ordered[flat:]], axis=1)
    rope_rows = arrived_ref[:, 2 * row_tiles].reshape(devices * 8, 128)
    ordered = jnp.dot(rope_order_ref[...], rope_rows, preferred_element_type=f32).astype(bf16)
    rope_query = jnp.concatenate([ordered[:flat], ordered[flat:]], axis=1)
    query_ref[...] = query
    rope_query_ref[...] = rope_query
    limits = limit_ref[...][:, 0:1]
    blocks = ((own_ref[...], own_rope_ref[...]), (core_ref[...], core_rope_ref[...]))
    for index, (keys, rope_keys) in enumerate(blocks):
        begin = lax.bitwise_xor(me, index) * block_len
        scores_ref[index] = score_block(query, rope_query, keys, rope_keys, begin, limits, heads_each)


def attend(heads_each, query_ref, rope_query_ref, scores_ref, limit_ref, own_ref, core_ref, near_ref, far_ref, near_rope_ref, far_rope_ref, out_ref, more_ref):
    flat, _ = query_ref.shape
    total_rows = flat // heads_each
    block_len = own_ref.shape[0]
    me = lax.axis_index("ctx")
    limits = limit_ref[...][:, 0:1]
    query, rope_query = query_ref[...], rope_query_ref[...]
    core = lax.rem(me, 2)
    owners = [me, lax.bitwise_xor(me, 1), lax.bitwise_xor(me, 2 + 2 * core), lax.bitwise_xor(me, 5 - 2 * core)]
    highest = jnp.maximum(
        jnp.max(scores_ref[0], axis=1, keepdims=True), jnp.max(scores_ref[1], axis=1, keepdims=True)
    )
    for index, (block, rope_block) in enumerate(((near_ref, near_rope_ref), (far_ref, far_rope_ref))):
        begin = owners[index + 2] * block_len
        scores = score_block(query, rope_query, block[...], rope_block[...], begin, limits, heads_each)
        more_ref[index] = scores
        highest = jnp.maximum(highest, jnp.max(scores, axis=1, keepdims=True))
    highest = jnp.maximum(highest, no_position)
    total = None
    summed = None
    for index, block in enumerate((own_ref, core_ref, near_ref, far_ref)):
        scores = scores_ref[index] if index < 2 else more_ref[index - 2]
        weights = jnp.exp2((scores - highest) * exponent_scale).astype(bf16)
        part = jnp.sum(weights.astype(f32), axis=1, keepdims=True)
        summed = part if summed is None else summed + part
        part = jnp.dot(weights, block[...], preferred_element_type=f32)
        total = part if total is None else total + part
    lane = lax.broadcasted_iota(jnp.int32, (8, 128), 1)
    for head in range(heads_each):
        base = head * total_rows
        out_ref[head, 0:total_rows, :] = total[base : base + total_rows].astype(bf16)
        note = jnp.zeros((8, 128), f32)
        for tile in range(total_rows // 8):
            for offset, value in ((0, highest), (3, summed)):
                value = jnp.broadcast_to(value[base + tile * 8 : base + tile * 8 + 8], (8, 128))
                for piece in range(3):
                    rounded = value.astype(bf16).astype(f32)
                    note = jnp.where(lane == 8 * tile + offset + piece, rounded, note)
                    value = value - rounded
        wide = jnp.concatenate([note, jnp.zeros((8, out_ref.shape[2] - 128), f32)], axis=1)
        out_ref[head, total_rows:, :] = wide.astype(bf16)


def merge_project(arrived_ref, weight_ref, own_ref, other_ref, attention_ref, product_ref):
    sources, height, _ = arrived_ref.shape
    total_rows = height - 8
    peaks = []
    sums = []
    for source in range(sources):
        note = arrived_ref[source, total_rows:, 0:128].astype(f32)
        shifted = [note] + [pltpu.roll(note, 128 - step, 1) for step in range(1, 6)]
        peaks.append(shifted[0] + shifted[1] + shifted[2])
        sums.append(shifted[3] + shifted[4] + shifted[5])
    highest = functools.reduce(jnp.maximum, peaks)
    factors = [jnp.exp2((peak - highest) * exponent_scale) for peak in peaks]
    divisor = sum(factor * part for factor, part in zip(factors, sums))
    factors = [factor / divisor for factor in factors]
    for tile in range(total_rows // 8):
        span = slice(tile * 8, tile * 8 + 8)
        attention_ref[span, :] = sum(
            factor[:, 8 * tile : 8 * tile + 1] * arrived_ref[source, span, :].astype(f32)
            for source, factor in enumerate(factors)
        )
    product = jnp.dot(attention_ref[...].astype(bf16), weight_ref[...], preferred_element_type=f32)
    product_ref[...] = product.reshape(product_ref.shape)
    core = lax.rem(lax.axis_index("ctx"), 2)
    own_ref[...] = product_ref[core]
    other_ref[...] = product_ref[1 - core].astype(bf16)


def strips_of(array):
    return jnp.concatenate(
        [array[:, part * strip : (part + 1) * strip] for part in range(array.shape[1] // strip)], axis=0
    )


def combine(own_ref, other_ref, order_ref, out_ref):
    summed = strips_of(own_ref[...] + other_ref[...].astype(f32)).astype(bf16)
    ordered = jnp.dot(order_ref[...], summed, preferred_element_type=f32).astype(bf16)
    out_ref[...] = ordered.reshape(out_ref.shape)


def norm_rows(arrived_ref, residual_ref, gain_ref, projected_ref, hidden_ref, out_ref, natural, stripped):
    rows, width = residual_ref.shape
    strips = width // strip
    summed = jnp.sum(arrived_ref[...].astype(f32), axis=0)
    for row in range(rows):
        for part in range(strips):
            at = row * strips + part
            natural[row : row + 1, part * strip : (part + 1) * strip] = summed[at : at + 1]
    projected = natural[0:rows, :]
    projected_ref[...] = projected
    hidden = residual_ref[...].astype(f32) + projected
    hidden_ref[...] = hidden
    scale = lax.rsqrt(jnp.mean(hidden * hidden, axis=1, keepdims=True) + norm_eps)
    normed = hidden * scale * gain_ref[...].reshape(1, width)
    stripped[...] = jnp.zeros_like(stripped)
    for row in range(rows):
        for part in range(strips):
            at = row * strips + part
            stripped[at : at + 1, :] = normed[row : row + 1, part * strip : (part + 1) * strip]
    tile = stripped[...].astype(bf16)
    for chip in range(out_ref.shape[0]):
        out_ref[chip] = tile


def run_expert(rows, own_rows_ref, other_rows_ref, back_ref, ids_ref, route_ref, gate_ref, up_ref, down_ref, own_ref, other_ref):
    chips, height, _ = own_rows_ref.shape
    half_rows = chips * rows
    strips = gate_ref.shape[0] // strip
    me = lax.axis_index("ctx")
    ordered = [
        jnp.dot(back_ref[...], ref[...].reshape(chips * height, strip), preferred_element_type=f32)
        for ref in (own_rows_ref, other_rows_ref)
    ]
    inputs = jnp.concatenate(
        [
            jnp.concatenate([part[at * half_rows : (at + 1) * half_rows] for part in ordered], axis=0)
            for at in range(strips)
        ],
        axis=1,
    ).astype(bf16)
    row = lax.broadcasted_iota(jnp.int32, (1, 2 * half_rows), 1)
    device = sum((row >= step * rows).astype(jnp.int32) for step in range(1, 2 * chips))
    other = (lax.rem(device, 2) != lax.rem(me, 2)).astype(jnp.int32)
    target = other * half_rows + lax.shift_right_logical(device, 1) * rows + row - device * rows
    named = jnp.sum(jnp.where(ids_ref[...] == me, route_ref[...], 0.0), axis=0, keepdims=True)
    place = lax.broadcasted_iota(jnp.int32, (2 * half_rows, 2 * half_rows), 0)
    weight = jnp.sum(jnp.where(place == target, named, 0.0), axis=1, keepdims=True)
    gate = jnp.dot(inputs, gate_ref[...], preferred_element_type=f32)
    up = jnp.dot(inputs, up_ref[...], preferred_element_type=f32)
    hidden = (gate * (1.0 / (1.0 + jnp.exp(-gate))) * up).astype(bf16)
    result = jnp.dot(hidden, down_ref[...], preferred_element_type=f32)
    result = jnp.where(weight > 0.0, result * weight, 0.0)
    own_ref[...] = result[:half_rows]
    other_ref[...] = result[half_rows:].astype(bf16)


def add_mixture(arrived_ref, hidden_ref, projected_ref, attn_ref, out_ref, natural):
    rows, width = hidden_ref.shape
    strips = width // strip
    attn_ref[...] = projected_ref[...].astype(bf16)
    mixture = jnp.sum(arrived_ref[...].astype(f32), axis=0)
    for row in range(rows):
        for part in range(strips):
            at = row * strips + part
            natural[row : row + 1, part * strip : (part + 1) * strip] = mixture[at : at + 1]
    out_ref[...] = (hidden_ref[...] + natural[0:rows, :]).astype(bf16)


def kernel_layer(
    query_latent,
    query_rope,
    cache_latent,
    cache_rope,
    valid_len,
    w_vo,
    residual,
    norm_gain,
    expert_ids,
    route_weight,
    w_gate,
    w_up,
    w_down,
):
    devices = lax.axis_size("ctx")
    rows, width = residual.shape
    block_len, latent = cache_latent.shape
    rope_dim = cache_rope.shape[0]
    head_count = query_rope.shape[1] // rope_dim
    total_rows = rows * devices
    heads_each = head_count // share
    per = rows * heads_each
    strips = width // strip
    height = 8 * -(-rows * strips // 8)

    def swap(array):
        return lax.ppermute(array, "ctx", [(d, d ^ 1) for d in range(devices)])

    def trade(array):
        return lax.ppermute(array, "ctx", [(d, d ^ (2 + d % 2 * 2)) for d in range(devices)])

    tiles = 2 * per // 8 * 2 + 1
    flat = heads_each * total_rows
    outgoing = call(
        functools.partial(prepare, heads_each),
        jax.ShapeDtypeStruct((devices, tiles, 8, 128), bf16),
        query_latent,
        query_rope,
        spaces={0: pltpu.HBM, 1: pltpu.HBM},
        limit=60,
        scratch=[
            VMEM(query_latent.shape, bf16),
            VMEM(query_rope.shape, bf16),
            VMEM((share, 2 * per, latent // 2), f32),
            VMEM((share, 16, 128), f32),
            VMEM((share, tiles, 8, 128), bf16),
            pltpu.SemaphoreType.DMA((2,)),
            pltpu.SemaphoreType.DMA((devices,)),
        ],
        out_space=pl.ANY,
    )
    near = trade(cache_latent)
    rope, outgoing = lax.optimization_barrier((cache_rope, outgoing))
    core = swap(cache_latent)
    core_rope = swap(rope)
    near_rope = trade(rope)
    arrived = lax.all_to_all(outgoing, "ctx", split_axis=0, concat_axis=0, tiled=True)
    order, rope_order, limits = call(
        functools.partial(tables, rows, heads_each),
        (
            jax.ShapeDtypeStruct((2 * flat, 2 * per // 8 * devices * 8), bf16),
            jax.ShapeDtypeStruct((2 * flat, devices * 8), bf16),
            jax.ShapeDtypeStruct((total_rows, 128), jnp.int32),
        ),
        valid_len,
        spaces={0: SMEM},
    )
    far_rope = swap(near_rope)
    near, core, core_rope, far_rope, order, rope_order, limits, arrived = lax.optimization_barrier(
        (near, core, core_rope, far_rope, order, rope_order, limits, arrived)
    )
    far = swap(near)
    query, rope_query, scores = call(
        functools.partial(score_near, heads_each),
        (
            jax.ShapeDtypeStruct((flat, latent), bf16),
            jax.ShapeDtypeStruct((flat, 256), bf16),
            jax.ShapeDtypeStruct((2, flat, block_len), f32),
        ),
        arrived,
        order,
        rope_order,
        limits,
        cache_latent,
        cache_rope,
        core,
        core_rope,
    )
    partial = call(
        functools.partial(attend, heads_each),
        jax.ShapeDtypeStruct((heads_each, total_rows + 8, latent), bf16),
        query,
        rope_query,
        scores,
        limits,
        cache_latent,
        core,
        near,
        far,
        near_rope,
        far_rope,
        scratch=[VMEM((2, flat, block_len), f32)],
    )
    lines = [[d for d in range(devices) if place(d) == kind] for kind in range(share)]
    chips = devices // 2
    half_rows = rows * chips
    same_core = [[2 * chip + c for chip in range(chips)] for c in range(2)]
    send = strip_order(rows, chips, strips, height)
    send_order, back_order = jnp.asarray(send, bf16), jnp.asarray(send.T, bf16)
    strip_shape = jax.ShapeDtypeStruct((chips, height, strip), bf16)
    halves = (
        jax.ShapeDtypeStruct((half_rows, width), f32),
        jax.ShapeDtypeStruct((half_rows, width), bf16),
    )

    def exchange(array, partners):
        return lax.all_to_all(array, "ctx", split_axis=0, concat_axis=0, axis_index_groups=partners, tiled=True)

    pieces = exchange(partial, lines)
    kept, given = call(
        merge_project,
        halves,
        pieces,
        w_vo,
        scratch=[VMEM((total_rows, latent), f32), VMEM((2, half_rows, width), f32)],
    )
    columns = call(combine, strip_shape, kept, swap(given), send_order)
    projected, hidden_state, normed = call(
        norm_rows,
        (
            jax.ShapeDtypeStruct((rows, width), f32),
            jax.ShapeDtypeStruct((rows, width), f32),
            strip_shape,
        ),
        exchange(columns, same_core),
        residual,
        norm_gain,
        scratch=[VMEM((8, width), f32), VMEM((height, strip), f32)],
    )
    inputs = exchange(normed, same_core)
    kept, given = call(
        functools.partial(run_expert, rows),
        halves,
        inputs,
        swap(inputs),
        back_order,
        expert_ids.T,
        route_weight.T,
        w_gate[0],
        w_up[0],
        w_down[0],
    )
    results = call(combine, strip_shape, kept, swap(given), send_order)
    attn_out, layer_out = call(
        add_mixture,
        (jax.ShapeDtypeStruct((rows, width), bf16), jax.ShapeDtypeStruct((rows, width), bf16)),
        exchange(results, same_core),
        hidden_state,
        projected,
        scratch=[VMEM((8, width), f32)],
    )
    return attn_out, layer_out


def fits(mesh, query_rope, residual, cache_latent, cache_rope):
    devices = mesh.shape["ctx"]
    rope_dim = cache_rope.shape[0] // mesh.shape["groups"]
    heads = query_rope.shape[1] // rope_dim
    rows = residual.shape[0] // (devices * mesh.shape["groups"])
    per = rows * heads // share
    return (
        heads == devices
        and devices % (2 * share) == 0
        and rope_dim == 64
        and 2 * per % 8 == 0
        and 8 <= per <= 16
        and rows * devices % 16 == 0
        and rows * devices <= 128
        and cache_latent.shape[1] == 512
        and cache_latent.shape[0] // (devices * mesh.shape["groups"]) == 512
        and devices & (devices - 1) == 0
        and residual.shape[1] % strip == 0
    )


def solution(mesh):
    in_specs = (
        P(("groups", "ctx"), None),
        P(("groups", "ctx"), None),
        P(("groups", "ctx"), None),
        P("groups", "ctx"),
        P("groups"),
        P("ctx", None),
        P(("groups", "ctx"), None),
        P(),
        P("groups", None),
        P("groups", None),
        P("ctx", None, None),
        P("ctx", None, None),
        P("ctx", None, None),
    )
    out_specs = (P(("groups", "ctx"), None), P(("groups", "ctx"), None))

    def layer(*args):
        kernels = fits(mesh, args[1], args[6], args[2], args[3])

        def body(*shards):
            return (kernel_layer if kernels else plain_layer)(*shards)

        step = jax.shard_map(body, mesh=mesh, in_specs=in_specs, out_specs=out_specs, check_vma=False)
        return step(*args)

    return layer
```

profile of v0, /device:TPU:0, one launch (start us, length us, event | category | flops | bytes accessed | tf_op | source)
XLA Modules:
  0.0 75.2 jit_solution(4231387306226542148)
XLA Ops:
  0.6 0.0 copy-start.5
  0.6 0.0 copy-start.10
  0.7 0.6 collective-permute-start.1
  1.2 2.6 %collective-permute-start = (bf16[512,512]{1,0:T(8,128)(2,1)}, bf16[512,512]{1,0:T(8,128)(2,1)S(1)}, u32[]{:S(2)}, u32[]{:S(2)}) collective-permute-start(bf16[512,512]{1,0:T(8,128)(2,1)} %own_ref.3), channel_id=1, source_target_pairs={{0,2},{1,5},{2,0},{3,7},{4,6},{5,1},{6,4},{7,3},{8,10},{9,13},{10,... | collective-permute-start | bytes 1572872 | tf_op jit(solution)/shard_map/ppermute | solution.py:459
  3.8 1.8 %shard_map.158 = bf16[16,7,8,128]{3,2,1,0:T(8,128)(2,1)} custom-call(bf16[3,8192]{1,0:T(4,128)(2,1)} %query_hbm.1, bf16[3,1024]{1,0:T(4,128)(2,1)} %rope_hbm.1), custom_call_target="tpu_custom_call" | custom-call | flops 4000000000 | bytes 67108864 | tf_op jit(solution)/shard_map/pallas_call | solution.py:133
  5.6 0.0 copy-done.5
  5.6 0.1 collective-permute-start.3
  5.7 6.4 %all-to-all-start = ((bf16[16,7,8,128]{3,2,1,0:T(8,128)(2,1)}), bf16[16,7,8,128]{3,2,1,0:T(8,128)(2,1)S(1)}, u32[]{:S(2)}, u32[]{:S(2)}) async-start(bf16[16,7,8,128]{3,2,1,0:T(8,128)(2,1)} %shard_map.158), calls=%async_computation | async-start | bytes 458752 | tf_op jit(solution)/shard_map/all_to_all | solution.py:486
  12.1 0.0 copy-start.4
  12.1 0.5 collective-permute-start.2
  12.6 0.0 collective-permute-done.3.near_rope_ref
  12.6 0.1 collective-permute-start.4
  12.7 0.0 copy-done.10
  12.7 0.6 shard_map.159
  13.4 0.1 collective-permute-done.2.core_rope_ref
  13.5 0.4 collective-permute-done.4.far_rope_ref
  13.9 7.7 %all-to-all-done.arrived_ref = bf16[16,7,8,128]{3,2,1,0:T(8,128)(2,1)S(1)} async-done(((bf16[16,7,8,128]{3,2,1,0:T(8,128)(2,1)}), bf16[16,7,8,128]{3,2,1,0:T(8,128)(2,1)S(1)}, u32[]{:S(2)}, u32[]{:S(2)}) %all-to-all-start) | async-done | bytes 229408 | tf_op jit(solution)/shard_map/all_to_all | solution.py:486
  21.6 0.0 collective-permute-done.1.core_ref
  21.6 0.0 collective-permute-done.near_ref
  21.6 0.0 collective-permute-start.5
  21.6 0.0 copy-done.4
  21.6 0.9 %shard_map.160 = (bf16[192,512]{1,0:T(8,128)(2,1)S(1)}, bf16[192,256]{1,0:T(8,128)(2,1)S(1)}, f32[2,192,512]{2,1,0:T(8,128)S(1)}) custom-call(bf16[16,7,8,128]{3,2,1,0:T(8,128)(2,1)S(1)} %all-to-all-done.arrived_ref, bf16[384,384]{1,0:T(8,128)(2,1)S(1)} %get-tuple-element.31.order_ref, bf16[384,128]{1,0:T(8,128)(2,1)S(1)} %get-tuple-element.32.rope_order_ref, ...), custom_call_target="tpu_custom_call" | custom-call | flops 4000000000 | bytes 67108864 | tf_op jit(solution)/shard_map/pallas_call | solution.py:133
  22.5 1.0 %collective-permute-done.5.far_ref = bf16[512,512]{1,0:T(8,128)(2,1)S(1)} collective-permute-done((bf16[512,512]{1,0:T(8,128)(2,1)S(1)}, bf16[512,512]{1,0:T(8,128)(2,1)S(1)}, u32[]{:S(2)}, u32[]{:S(2)}) %collective-permute-start.5) | collective-permute-done | bytes 524320 | tf_op jit(solution)/shard_map/ppermute | solution.py:456
  23.5 1.4 %shard_map.161 = bf16[4,56,512]{2,1,0:T(8,128)(2,1)S(1)} custom-call(bf16[192,512]{1,0:T(8,128)(2,1)S(1)} %get-tuple-element.36.query_ref, bf16[192,256]{1,0:T(8,128)(2,1)S(1)} %get-tuple-element.37.rope_query_ref, f32[2,192,512]{2,1,0:T(8,128)S(1)} %get-tuple-element.38.scores_ref, s32[48,128]{1,0:T(8,128)S(1)} %get-tuple-element.33.limit_ref, ...), custom_call_target="tpu_custom_call" | custom-call | flops 4000000000 | bytes 67108864 | tf_op jit(solution)/shard_map/pallas_call | solution.py:133
  24.9 11.3 %all_to_all.25.arrived_ref = bf16[4,56,512]{2,1,0:T(8,128)(2,1)S(1)} all-to-all(bf16[4,56,512]{2,1,0:T(8,128)(2,1)S(1)} %shard_map.161), channel_id=1, replica_groups={{0,6,8,14},{1,7,9,15},{2,4,10,12},{3,5,11,13},{16,22,24,30},{17,23,25,3..., dimensions={0} | all-to-all | bytes 458752 | tf_op jit(solution)/shard_map/all_to_all | solution.py:546
  36.2 0.0 copy-done.3
  36.2 0.7 shard_map.162
  36.9 0.1 collective-permute-start.6
  37.0 1.3 %collective-permute-done.6.other_ref = bf16[24,2560]{1,0:T(8,128)(2,1)S(1)} collective-permute-done((bf16[24,2560]{1,0:T(8,128)(2,1)S(1)}, bf16[24,2560]{1,0:T(8,128)(2,1)S(1)}, u32[]{:S(2)}, u32[]{:S(2)}) %collective-permute-start.6) | collective-permute-done | bytes 122912 | tf_op jit(solution)/shard_map/ppermute | solution.py:456
  38.3 0.0 copy-done.11
  38.3 0.2 shard_map.163
  38.5 10.3 %all_to_all.26.arrived_ref = bf16[8,16,512]{2,1,0:T(8,128)(2,1)S(1)} all-to-all(bf16[8,16,512]{2,1,0:T(8,128)(2,1)S(1)} %shard_map.163), channel_id=1, replica_groups={{0,2,4,6,8,10,12,14},{1,3,5,7,9,11,13,15},{16,18,20,22,24,26,28,30},{17..., dimensions={0} | all-to-all | bytes 262144 | tf_op jit(solution)/shard_map/all_to_all | solution.py:546
  48.8 0.0 copy-done.6
  48.8 0.0 copy-start.2
  48.8 0.0 copy-start.8
  48.9 0.0 copy-start.9
  48.9 0.0 copy-start.12
  48.9 0.2 shard_map.164
  49.0 10.3 %all_to_all.27.own_rows_ref = bf16[8,16,512]{2,1,0:T(8,128)(2,1)S(1)} all-to-all(bf16[8,16,512]{2,1,0:T(8,128)(2,1)S(1)} %get-tuple-element.43), channel_id=1, replica_groups={{0,2,4,6,8,10,12,14},{1,3,5,7,9,11,13,15},{16,18,20,22,24,26,28,30},{17..., dimensions={0} | all-to-all | bytes 262144 | tf_op jit(solution)/shard_map/all_to_all | solution.py:546
  59.3 0.0 collective-permute-start.7
  59.3 1.3 %collective-permute-done.7.other_rows_ref = bf16[8,16,512]{2,1,0:T(8,128)(2,1)S(1)} collective-permute-done((bf16[8,16,512]{2,1,0:T(8,128)(2,1)S(1)}, bf16[8,16,512]{2,1,0:T(8,128)(2,1)S(1)}, u32[]{:S(2)}, u32[]{:S(2)}) %collective-permute-start.7) | collective-permute-done | bytes 131104 | tf_op jit(solution)/shard_map/ppermute | solution.py:456
  60.7 0.0 copy-done
  60.7 2.3 %shard_map.165 = (f32[24,2560]{1,0:T(8,128)S(1)}, bf16[24,2560]{1,0:T(8,128)(2,1)S(1)}) custom-call(bf16[8,16,512]{2,1,0:T(8,128)(2,1)S(1)} %all_to_all.27.own_rows_ref, bf16[8,16,512]{2,1,0:T(8,128)(2,1)S(1)} %collective-permute-done.7.other_rows_ref, bf16[120,128]{1,0:T(8,128)(2,1)S(1)} %copy-done.12, s32[6,48]{1,0:T(8,128)S(1)} %bitcast.8, ...), custom_call_target="tpu_custom_call" | custom-call | flops 4000000000 | bytes 67108864 | tf_op jit(solution)/shard_map/pallas_call | solution.py:133
  63.0 0.2 collective-permute-start.8
  63.2 1.2 %collective-permute-done.8.other_ref = bf16[24,2560]{1,0:T(8,128)(2,1)S(1)} collective-permute-done((bf16[24,2560]{1,0:T(8,128)(2,1)S(1)}, bf16[24,2560]{1,0:T(8,128)(2,1)S(1)}, u32[]{:S(2)}, u32[]{:S(2)}) %collective-permute-start.8) | collective-permute-done | bytes 122912 | tf_op jit(solution)/shard_map/ppermute | solution.py:456
  64.4 0.2 shard_map.166
  64.6 10.0 %all_to_all.28.arrived_ref = bf16[8,16,512]{2,1,0:T(8,128)(2,1)S(1)} all-to-all(bf16[8,16,512]{2,1,0:T(8,128)(2,1)S(1)} %shard_map.166), channel_id=1, replica_groups={{0,2,4,6,8,10,12,14},{1,3,5,7,9,11,13,15},{16,18,20,22,24,26,28,30},{17..., dimensions={0} | all-to-all | bytes 262144 | tf_op jit(solution)/shard_map/all_to_all | solution.py:546
  74.6 0.7 shard_map.167
  (12 shorter events, 0.0 us)
Async XLA Ops:
  0.6 5.0 %copy-start.5 = (bf16[64,512]{1,0:T(8,128)(2,1)S(1)}, bf16[64,512]{1,0:T(8,128)(2,1)}, u32[]{:S(2)}) copy-start(bf16[64,512]{1,0:T(8,128)(2,1)} %own_rope_ref.1) | copy-start | bytes 196612
  0.6 12.1 %copy-start.10 = (s32[48]{0:T(128)S(1)}, s32[48]{0:T(128)}, u32[]{:S(2)}) copy-start(s32[48]{0:T(128)} %length_ref.1) | copy-start | bytes 580
  0.7 21.0 %collective-permute-start.1 = (bf16[512,512]{1,0:T(8,128)(2,1)}, bf16[512,512]{1,0:T(8,128)(2,1)S(1)}, u32[]{:S(2)}, u32[]{:S(2)}) collective-permute-start(bf16[512,512]{1,0:T(8,128)(2,1)} %own_ref.3), channel_id=1, source_target_pairs={{0,1},{1,0},{2,3},{3,2},{4,5},{5,4},{6,7},{7,6},{8,9},{9,8},{10,11... | collective-permute-start | bytes 1572872 | tf_op jit(solution)/shard_map/ppermute | solution.py:456
  1.2 20.4 %collective-permute-start = (bf16[512,512]{1,0:T(8,128)(2,1)}, bf16[512,512]{1,0:T(8,128)(2,1)S(1)}, u32[]{:S(2)}, u32[]{:S(2)}) collective-permute-start(bf16[512,512]{1,0:T(8,128)(2,1)} %own_ref.3), channel_id=1, source_target_pairs={{0,2},{1,5},{2,0},{3,7},{4,6},{5,1},{6,4},{7,3},{8,10},{9,13},{10,... | collective-permute-start | bytes 1572872 | tf_op jit(solution)/shard_map/ppermute | solution.py:459
  5.6 7.0 %collective-permute-start.3 = (bf16[64,512]{1,0:T(8,128)(2,1)S(1)}, bf16[64,512]{1,0:T(8,128)(2,1)S(1)}, u32[]{:S(2)}, u32[]{:S(2)}) collective-permute-start(bf16[64,512]{1,0:T(8,128)(2,1)S(1)} %copy-done.5), channel_id=1, source_target_pairs={{0,2},{1,5},{2,0},{3,7},{4,6},{5,1},{6,4},{7,3},{8,10},{9,13},{10,... | collective-permute-start | bytes 196616 | tf_op jit(solution)/shard_map/ppermute | solution.py:459
  5.7 15.9 %all-to-all-start = ((bf16[16,7,8,128]{3,2,1,0:T(8,128)(2,1)}), bf16[16,7,8,128]{3,2,1,0:T(8,128)(2,1)S(1)}, u32[]{:S(2)}, u32[]{:S(2)}) async-start(bf16[16,7,8,128]{3,2,1,0:T(8,128)(2,1)} %shard_map.158), calls=%async_computation | async-start | bytes 458752 | tf_op jit(solution)/shard_map/all_to_all | solution.py:486
  12.1 9.5 %copy-start.4 = (bf16[512,512]{1,0:T(8,128)(2,1)S(1)}, bf16[512,512]{1,0:T(8,128)(2,1)}, u32[]{:S(2)}) copy-start(bf16[512,512]{1,0:T(8,128)(2,1)} %own_ref.3) | copy-start | bytes 1572868
  12.1 1.4 %collective-permute-start.2 = (bf16[64,512]{1,0:T(8,128)(2,1)S(1)}, bf16[64,512]{1,0:T(8,128)(2,1)S(1)}, u32[]{:S(2)}, u32[]{:S(2)}) collective-permute-start(bf16[64,512]{1,0:T(8,128)(2,1)S(1)} %copy-done.5), channel_id=1, source_target_pairs={{0,1},{1,0},{2,3},{3,2},{4,5},{5,4},{6,7},{7,6},{8,9},{9,8},{10,11... | collective-permute-start | bytes 196616 | tf_op jit(solution)/shard_map/ppermute | solution.py:456
  12.6 1.3 %collective-permute-start.4 = (bf16[64,512]{1,0:T(8,128)(2,1)S(1)}, bf16[64,512]{1,0:T(8,128)(2,1)S(1)}, u32[]{:S(2)}, u32[]{:S(2)}) collective-permute-start(bf16[64,512]{1,0:T(8,128)(2,1)S(1)} %collective-permute-done.3.near_rope_ref), channel_id=1, source_target_pairs={{0,1},{1,0},{2,3},{3,2},{4,5},{5,4},{6,7},{7,6},{8,9},{9,8},{10,11... | collective-permute-start | bytes 196616 | tf_op jit(solution)/shard_map/ppermute | solution.py:456
  21.6 1.9 %collective-permute-start.5 = (bf16[512,512]{1,0:T(8,128)(2,1)S(1)}, bf16[512,512]{1,0:T(8,128)(2,1)S(1)}, u32[]{:S(2)}, u32[]{:S(2)}) collective-permute-start(bf16[512,512]{1,0:T(8,128)(2,1)S(1)} %collective-permute-done.near_ref), channel_id=1, source_target_pairs={{0,1},{1,0},{2,3},{3,2},{4,5},{5,4},{6,7},{7,6},{8,9},{9,8},{10,11... | collective-permute-start | bytes 1572872 | tf_op jit(solution)/shard_map/ppermute | solution.py:456
  23.5 12.7 %copy-start.3 = (bf16[512,2560]{1,0:T(8,128)(2,1)S(1)}, bf16[512,2560]{1,0:T(8,128)(2,1)}, u32[]{:S(2)}) copy-start(bf16[512,2560]{1,0:T(8,128)(2,1)} %weight_ref.1) | copy-start | bytes 7864324
  36.2 2.1 %copy-start.11 = (bf16[128,120]{1,0:T(8,128)(2,1)S(1)}, bf16[128,120]{1,0:T(8,128)(2,1)}, u32[]{:S(2)}) copy-start(bf16[128,120]{1,0:T(8,128)(2,1)} %constant.4.clone.order_ref) | copy-start | bytes 92164
  36.9 1.4 %collective-permute-start.6 = (bf16[24,2560]{1,0:T(8,128)(2,1)S(1)}, bf16[24,2560]{1,0:T(8,128)(2,1)S(1)}, u32[]{:S(2)}, u32[]{:S(2)}) collective-permute-start(bf16[24,2560]{1,0:T(8,128)(2,1)S(1)} %get-tuple-element.42), channel_id=1, source_target_pairs={{0,1},{1,0},{2,3},{3,2},{4,5},{5,4},{6,7},{7,6},{8,9},{9,8},{10,11... | collective-permute-start | bytes 368648 | tf_op jit(solution)/shard_map/ppermute | solution.py:456
  38.3 10.5 %copy-start.6 = (bf16[3,2560]{1,0:T(4,128)(2,1)S(1)}, bf16[3,2560]{1,0:T(4,128)(2,1)}, u32[]{:S(2)}) copy-start(bf16[3,2560]{1,0:T(4,128)(2,1)} %residual_ref.1) | copy-start | bytes 46084
  38.3 10.5 %copy-start.7 = (f32[2560]{0:T(1024)S(1)}, f32[2560]{0:T(1024)}, u32[]{:S(2)}) copy-start(f32[2560]{0:T(1024)} %gain_ref.1) | copy-start | bytes 30724
  48.8 11.8 %copy-start = (bf16[1,2560,768]{2,1,0:T(8,128)(2,1)S(1)}, bf16[1,2560,768]{2,1,0:T(8,128)(2,1)}, u32[]{:S(2)}) copy-start(bf16[1,2560,768]{2,1,0:T(8,128)(2,1)} %param.25) | copy-start | bytes 11796484
  48.8 11.8 %copy-start.1 = (bf16[1,2560,768]{2,1,0:T(8,128)(2,1)S(1)}, bf16[1,2560,768]{2,1,0:T(8,128)(2,1)}, u32[]{:S(2)}) copy-start(bf16[1,2560,768]{2,1,0:T(8,128)(2,1)} %param.26) | copy-start | bytes 11796484
  48.8 11.8 %copy-start.2 = (bf16[1,768,2560]{2,1,0:T(8,128)(2,1)S(1)}, bf16[1,768,2560]{2,1,0:T(8,128)(2,1)}, u32[]{:S(2)}) copy-start(bf16[1,768,2560]{2,1,0:T(8,128)(2,1)} %param.27) | copy-start | bytes 11796484
  48.8 11.8 %copy-start.8 = (s32[48,6]{0,1:T(8,128)S(1)}, s32[48,6]{0,1:T(8,128)}, u32[]{:S(2)}) copy-start(s32[48,6]{0,1:T(8,128)} %param.23) | copy-start | bytes 3460
  48.9 11.8 %copy-start.9 = (f32[48,6]{0,1:T(8,128)S(1)}, f32[48,6]{0,1:T(8,128)}, u32[]{:S(2)}) copy-start(f32[48,6]{0,1:T(8,128)} %param.24) | copy-start | bytes 3460
  48.9 11.8 %copy-start.12 = (bf16[120,128]{1,0:T(8,128)(2,1)S(1)}, bf16[120,128]{1,0:T(8,128)(2,1)}, u32[]{:S(2)}) copy-start(bf16[120,128]{1,0:T(8,128)(2,1)} %constant.5.clone.back_ref) | copy-start | bytes 92164
  59.3 1.3 %collective-permute-start.7 = (bf16[8,16,512]{2,1,0:T(8,128)(2,1)S(1)}, bf16[8,16,512]{2,1,0:T(8,128)(2,1)S(1)}, u32[]{:S(2)}, u32[]{:S(2)}) collective-permute-start(bf16[8,16,512]{2,1,0:T(8,128)(2,1)S(1)} %all_to_all.27.own_rows_ref), channel_id=1, source_target_pairs={{0,1},{1,0},{2,3},{3,2},{4,5},{5,4},{6,7},{7,6},{8,9},{9,8},{10,11... | collective-permute-start | bytes 393224 | tf_op jit(solution)/shard_map/ppermute | solution.py:456
  63.0 1.4 %collective-permute-start.8 = (bf16[24,2560]{1,0:T(8,128)(2,1)S(1)}, bf16[24,2560]{1,0:T(8,128)(2,1)S(1)}, u32[]{:S(2)}, u32[]{:S(2)}) collective-permute-start(bf16[24,2560]{1,0:T(8,128)(2,1)S(1)} %get-tuple-element.45), channel_id=1, source_target_pairs={{0,1},{1,0},{2,3},{3,2},{4,5},{5,4},{6,7},{7,6},{8,9},{9,8},{10,11... | collective-permute-start | bytes 368648 | tf_op jit(solution)/shard_map/ppermute | solution.py:456
where the time goes:
time: 75.6 us; the launch traced here: 75.2 us
  blocking collectives  41.8 us (55%)
  waiting for transfers between devices  13.1 us (17%)
  starting transfers between devices  10.5 us (14%)
  Pallas kernels  8.89 us (12%)
  between operations  0.84 us (1%)
    all_to_all x4, blocking collectives, exchange(): lax.all_to_all(array, 'ctx', split_axis=0, concat_axis=0, axis_index_grou...  41.8 us
    pallas_call x10, Pallas kernels, call(): pl.pallas_call(kernel, out_shape=out_shape, in_specs=in_specs, out_specs=...  8.89 us
    all_to_all x1, waiting for transfers between devices, kernel_layer(): lax.all_to_all(outgoing, 'ctx', split_axis=0, concat_axis=0, tiled=True)  7.74 us
    all_to_all x1, starting transfers between devices, kernel_layer(): lax.all_to_all(outgoing, 'ctx', split_axis=0, concat_axis=0, tiled=True)  6.43 us
    ppermute x7, waiting for transfers between devices, swap(): return lax.ppermute(array, 'ctx', [(d, d ^ 1) for d in range(devices)])  5.39 us
    ppermute x2, starting transfers between devices, trade(): lax.ppermute(array, 'ctx', [(d, d ^ 2 + d % 2 * 2) for d in range(devices)])  2.66 us
  transfers between devices with their start and end apart: 10, of which 7 were waited for; matrix products, arithmetic and copies ran while one was open for 0% of the time, Pallas kernels for 4%

commit v1 on v0

--- a/solution.py
+++ b/solution.py
@@ -150,26 +150,25 @@
     return order
 
 
-def prepare(heads_each, query_hbm, rope_hbm, out_hbm, query_ref, rope_ref, piece, rope_piece, packed, arrive, leave):
-    fetches = [
+def prepare(heads_each, query_hbm, rope_hbm, out_ref, query_ref, rope_ref, piece, rope_piece, arrive):
+    copies = [
         pltpu.make_async_copy(query_hbm, query_ref, arrive.at[0]),
         pltpu.make_async_copy(rope_hbm, rope_ref, arrive.at[1]),
     ]
-    for fetch in fetches:
-        fetch.start()
+    for copy in copies:
+        copy.start()
     rows = query_ref.shape[0]
     per = rows * heads_each
     latent = query_ref.shape[1] // (heads_each * share)
     rope_dim = rope_ref.shape[1] // (heads_each * share)
     half_width = latent // 2
-    devices = out_hbm.shape[0]
+    devices = out_ref.shape[0]
     lane = lax.broadcasted_iota(jnp.int32, (8, 128), 1)
     rope_piece[...] = jnp.zeros_like(rope_piece)
-    for fetch in fetches:
-        fetch.wait()
+    for copy in copies:
+        copy.wait()
     query = query_ref[...].astype(f32)
     rope = rope_ref[...].astype(f32)
-    sends = []
     for kind in range(share):
         owners = [device for device in range(devices) if place(device) == kind]
         for item in range(per):
@@ -180,24 +179,23 @@
                 piece[kind, half * per + item : half * per + item + 1, :] = query[row : row + 1, begin : begin + half_width]
             block = head * rope_dim // 128
             rope_piece[kind, item : item + 1, :] = rope[row : row + 1, block * 128 : (block + 1) * 128]
+    for kind in range(share):
         first = rope_piece[kind, 0:8, :]
         second = rope_piece[kind, 8:16, :]
         if kind % 2 == 1:
             first = pltpu.roll(first, 64, 1)
         else:
             second = pltpu.roll(second, 64, 1)
-        row_tiles, lane_tiles = 2 * per // 8, half_width // 128
-        for rt in range(row_tiles):
-            for lt in range(lane_tiles):
-                tile = piece[kind, rt * 8 : (rt + 1) * 8, lt * 128 : (lt + 1) * 128]
-                packed[kind, rt * lane_tiles + lt] = tile.astype(bf16)
-        packed[kind, row_tiles * lane_tiles] = jnp.where(lane < 64, first, second).astype(bf16)
-        for device in owners:
-            send = pltpu.make_async_copy(packed.at[kind], out_hbm.at[device], leave.at[device])
-            send.start()
-            sends.append(send)
-    for send in sends:
-        send.wait()
+        tail = jnp.where(lane < 64, first, second).astype(bf16)
+        tiles = []
+        for rt in range(2 * per // 8):
+            for lt in range(half_width // 128):
+                tiles.append(piece[kind, rt * 8 : (rt + 1) * 8, lt * 128 : (lt + 1) * 128].astype(bf16))
+        tiles.append(tail)
+        for device in range(devices):
+            if place(device) == kind:
+                for index, tile in enumerate(tiles):
+                    out_ref[device, index] = tile
 
 
 def place_of(item, source, rows, heads_each, total_rows):
@@ -235,23 +233,29 @@
         rope_order_ref[half * flat : (half + 1) * flat, :] = one_hot(target, flat)
 
 
-def score_block(query, rope_query, keys, rope_keys, begin, limits, heads_each):
-    flat, _ = query.shape
+def score_block(query, rope_query, block_ref, rope_block_ref, owner, limits, heads_each):
+    flat = query.shape[0]
     total_rows = flat // heads_each
-    block_len = rope_keys.shape[1]
+    width = rope_block_ref.shape[1]
+    rope_keys = rope_block_ref[...]
     empty = jnp.zeros_like(rope_keys)
     rope_keys = jnp.concatenate([rope_keys, empty, empty, rope_keys], axis=0)
-    scores = lax.dot_general(query, keys, (((1,), (1,)), ((), ())), preferred_element_type=f32)
+    scores = lax.dot_general(query, block_ref[...], (((1,), (1,)), ((), ())), preferred_element_type=f32)
     scores = scores + jnp.dot(rope_query, rope_keys, preferred_element_type=f32)
-    valid = lax.broadcasted_iota(jnp.int32, (total_rows, block_len), 1) + begin < limits
-    return jnp.where(valid[None], scores.reshape(heads_each, total_rows, block_len), negative_fill).reshape(flat, block_len)
-
-
-def score_near(heads_each, arrived_ref, order_ref, rope_order_ref, limit_ref, own_ref, own_rope_ref, core_ref, core_rope_ref, query_ref, rope_query_ref, scores_ref):
+    valid = lax.broadcasted_iota(jnp.int32, (total_rows, width), 1) + owner * width < limits
+    return jnp.where(valid[None], scores.reshape(heads_each, total_rows, width), negative_fill).reshape(flat, width)
+
+
+def weigh(scores, highest, block_ref):
+    weights = jnp.exp2((scores - highest) * exponent_scale).astype(bf16)
+    summed = jnp.sum(weights.astype(f32), axis=1, keepdims=True)
+    return summed, jnp.dot(weights, block_ref[...], preferred_element_type=f32)
+
+
+def attend_three(heads_each, arrived_ref, order_ref, rope_order_ref, limit_ref, own_ref, own_rope_ref, core_ref, core_rope_ref, near_ref, near_rope_ref, query_ref, rope_query_ref, state_ref, total_ref, scores_ref):
     devices = arrived_ref.shape[0]
     flat = order_ref.shape[0] // 2
     row_tiles = arrived_ref.shape[1] // 2
-    block_len, _ = own_ref.shape
     me = lax.axis_index("ctx")
     gathered = jnp.concatenate(
         [
@@ -270,39 +274,33 @@
     query_ref[...] = query
     rope_query_ref[...] = rope_query
     limits = limit_ref[...][:, 0:1]
-    blocks = ((own_ref[...], own_rope_ref[...]), (core_ref[...], core_rope_ref[...]))
-    for index, (keys, rope_keys) in enumerate(blocks):
-        begin = lax.bitwise_xor(me, index) * block_len
-        scores_ref[index] = score_block(query, rope_query, keys, rope_keys, begin, limits, heads_each)
-
-
-def attend(heads_each, query_ref, rope_query_ref, scores_ref, limit_ref, own_ref, core_ref, near_ref, far_ref, near_rope_ref, far_rope_ref, out_ref, more_ref):
+    blocks = (own_ref, core_ref, near_ref)
+    rope_blocks = (own_rope_ref, core_rope_ref, near_rope_ref)
+    owners = (me, lax.bitwise_xor(me, 1), lax.bitwise_xor(me, 2 + 2 * lax.rem(me, 2)))
+    highest = jnp.full((flat, 1), no_position, f32)
+    for index, (block, rope_block, owner) in enumerate(zip(blocks, rope_blocks, owners)):
+        scores = score_block(query, rope_query, block, rope_block, owner, limits, heads_each)
+        scores_ref[index] = scores
+        highest = jnp.maximum(highest, jnp.max(scores, axis=1, keepdims=True))
+    parts = [weigh(scores_ref[index], highest, block) for index, block in enumerate(blocks)]
+    state_ref[0] = jnp.broadcast_to(highest, state_ref.shape[1:])
+    state_ref[1] = jnp.broadcast_to(sum(part[0] for part in parts), state_ref.shape[1:])
+    total_ref[...] = sum(part[1] for part in parts)
+
+
+def attend_last(heads_each, query_ref, rope_query_ref, state_ref, total_ref, limit_ref, far_ref, far_rope_ref, out_ref):
     flat, _ = query_ref.shape
     total_rows = flat // heads_each
-    block_len = own_ref.shape[0]
     me = lax.axis_index("ctx")
+    owner = lax.bitwise_xor(me, 5 - 2 * lax.rem(me, 2))
     limits = limit_ref[...][:, 0:1]
-    query, rope_query = query_ref[...], rope_query_ref[...]
-    core = lax.rem(me, 2)
-    owners = [me, lax.bitwise_xor(me, 1), lax.bitwise_xor(me, 2 + 2 * core), lax.bitwise_xor(me, 5 - 2 * core)]
-    highest = jnp.maximum(
-        jnp.max(scores_ref[0], axis=1, keepdims=True), jnp.max(scores_ref[1], axis=1, keepdims=True)
-    )
-    for index, (block, rope_block) in enumerate(((near_ref, near_rope_ref), (far_ref, far_rope_ref))):
-        begin = owners[index + 2] * block_len
-        scores = score_block(query, rope_query, block[...], rope_block[...], begin, limits, heads_each)
-        more_ref[index] = scores
-        highest = jnp.maximum(highest, jnp.max(scores, axis=1, keepdims=True))
-    highest = jnp.maximum(highest, no_position)
-    total = None
-    summed = None
-    for index, block in enumerate((own_ref, core_ref, near_ref, far_ref)):
-        scores = scores_ref[index] if index < 2 else more_ref[index - 2]
-        weights = jnp.exp2((scores - highest) * exponent_scale).astype(bf16)
-        part = jnp.sum(weights.astype(f32), axis=1, keepdims=True)
-        summed = part if summed is None else summed + part
-        part = jnp.dot(weights, block[...], preferred_element_type=f32)
-        total = part if total is None else total + part
+    scores = score_block(query_ref[...], rope_query_ref[...], far_ref, far_rope_ref, owner, limits, heads_each)
+    before = state_ref[0][:, 0:1]
+    highest = jnp.maximum(before, jnp.max(scores, axis=1, keepdims=True))
+    kept = jnp.exp2((before - highest) * exponent_scale)
+    summed, total = weigh(scores, highest, far_ref)
+    summed = summed + kept * state_ref[1][:, 0:1]
+    total = total + kept * total_ref[...]
     lane = lax.broadcasted_iota(jnp.int32, (8, 128), 1)
     for head in range(heads_each):
         base = head * total_rows
@@ -472,11 +470,8 @@
             VMEM(query_rope.shape, bf16),
             VMEM((share, 2 * per, latent // 2), f32),
             VMEM((share, 16, 128), f32),
-            VMEM((share, tiles, 8, 128), bf16),
             pltpu.SemaphoreType.DMA((2,)),
-            pltpu.SemaphoreType.DMA((devices,)),
         ],
-        out_space=pl.ANY,
     )
     near = trade(cache_latent)
     rope, outgoing = lax.optimization_barrier((cache_rope, outgoing))
@@ -494,17 +489,17 @@
         valid_len,
         spaces={0: SMEM},
     )
-    far_rope = swap(near_rope)
-    near, core, core_rope, far_rope, order, rope_order, limits, arrived = lax.optimization_barrier(
-        (near, core, core_rope, far_rope, order, rope_order, limits, arrived)
-    )
-    far = swap(near)
-    query, rope_query, scores = call(
-        functools.partial(score_near, heads_each),
+    near, near_rope, core, core_rope, order, rope_order, limits, arrived = lax.optimization_barrier(
+        (near, near_rope, core, core_rope, order, rope_order, limits, arrived)
+    )
+    far, far_rope = swap(near), swap(near_rope)
+    query, rope_query, state, total = call(
+        functools.partial(attend_three, heads_each),
         (
             jax.ShapeDtypeStruct((flat, latent), bf16),
             jax.ShapeDtypeStruct((flat, 256), bf16),
-            jax.ShapeDtypeStruct((2, flat, block_len), f32),
+            jax.ShapeDtypeStruct((2, flat, 128), f32),
+            jax.ShapeDtypeStruct((flat, latent), f32),
         ),
         arrived,
         order,
@@ -514,21 +509,20 @@
         cache_rope,
         core,
         core_rope,
+        near,
+        near_rope,
+        scratch=[VMEM((3, flat, block_len), f32)],
     )
     partial = call(
-        functools.partial(attend, heads_each),
+        functools.partial(attend_last, heads_each),
         jax.ShapeDtypeStruct((heads_each, total_rows + 8, latent), bf16),
         query,
         rope_query,
-        scores,
+        state,
+        total,
         limits,
-        cache_latent,
-        core,
-        near,
         far,
-        near_rope,
         far_rope,
-        scratch=[VMEM((2, flat, block_len), f32)],
     )
     lines = [[d for d in range(devices) if place(d) == kind] for kind in range(share)]
     chips = devices // 2

time: 75.6 us -> 74.5 us (0.985)
  waiting for transfers between devices: 13.1 us -> 11.1 us
    all_to_all x1, waiting for transfers between devices: 7.74 us -> 4.74 us  [kernel_layer(): lax.all_to_all(outgoing, 'ctx', split_axis=0, concat_axis=0, tiled=True)]
    ppermute x2, waiting for transfers between devices: 0.01 us -> 2.52 us  [trade(): lax.ppermute(array, 'ctx', [(d, d ^ 2 + d % 2 * 2) for d in range(devices)])]
    ppermute x2, starting transfers between devices: 2.66 us -> 4.69 us  [trade(): lax.ppermute(array, 'ctx', [(d, d ^ 2 + d % 2 * 2) for d in range(devices)])]
    ppermute x7, waiting for transfers between devices: 5.39 us -> 3.87 us  [swap(): return lax.ppermute(array, 'ctx', [(d, d ^ 1) for d in range(devices)])]
    all_to_all x1, starting transfers between devices: 6.43 us -> 5.11 us  [kernel_layer(): lax.all_to_all(outgoing, 'ctx', split_axis=0, concat_axis=0, tiled=True)]
  transfers between devices with their start and end apart: 10 -> 10, of which waited for: 7 -> 5; matrix products, arithmetic and copies ran while one was open for 0% -> 0% of each run, Pallas kernels for 4% -> 6%
where the time goes in v1:
time: 74.5 us; the launch traced here: 74.1 us
  blocking collectives  41.5 us (56%)
  starting transfers between devices  11.1 us (15%)
  waiting for transfers between devices  11.1 us (15%)
  Pallas kernels  9.49 us (13%)
  between operations  0.86 us (1%)
    all_to_all x4, blocking collectives, exchange(): lax.all_to_all(array, 'ctx', split_axis=0, concat_axis=0, axis_index_grou...  41.5 us
    pallas_call x10, Pallas kernels, call(): pl.pallas_call(kernel, out_shape=out_shape, in_specs=in_specs, out_specs=...  9.49 us
    all_to_all x1, starting transfers between devices, kernel_layer(): lax.all_to_all(outgoing, 'ctx', split_axis=0, concat_axis=0, tiled=True)  5.11 us
    all_to_all x1, waiting for transfers between devices, kernel_layer(): lax.all_to_all(outgoing, 'ctx', split_axis=0, concat_axis=0, tiled=True)  4.74 us
    ppermute x2, starting transfers between devices, trade(): lax.ppermute(array, 'ctx', [(d, d ^ 2 + d % 2 * 2) for d in range(devices)])  4.69 us
    ppermute x7, waiting for transfers between devices, swap(): return lax.ppermute(array, 'ctx', [(d, d ^ 1) for d in range(devices)])  3.87 us
    ppermute x2, waiting for transfers between devices, trade(): lax.ppermute(array, 'ctx', [(d, d ^ 2 + d % 2 * 2) for d in range(devices)])  2.52 us
  transfers between devices with their start and end apart: 10, of which 5 were waited for; matrix products, arithmetic and copies ran while one was open for 0% of the time, Pallas kernels for 6%

profile of v1, /device:TPU:0, one launch (start us, length us, event | category | flops | bytes accessed | tf_op | source)
XLA Modules:
  0.0 74.1 jit_solution(10816422434659622317)
XLA Ops:
  0.6 0.0 copy-start.5
  0.6 0.0 copy-start.10
  0.7 3.1 %collective-permute-start = (bf16[512,512]{1,0:T(8,128)(2,1)}, bf16[512,512]{1,0:T(8,128)(2,1)S(1)}, u32[]{:S(2)}, u32[]{:S(2)}) collective-permute-start(bf16[512,512]{1,0:T(8,128)(2,1)} %own_ref.1), channel_id=1, source_target_pairs={{0,2},{1,5},{2,0},{3,7},{4,6},{5,1},{6,4},{7,3},{8,10},{9,13},{10,... | collective-permute-start | bytes 1572872 | tf_op jit(solution)/shard_map/ppermute | solution.py:457
  3.7 0.0 collective-permute-start.2
  3.7 1.6 %shard_map.158 = bf16[16,7,8,128]{3,2,1,0:T(8,128)(2,1)} custom-call(bf16[3,8192]{1,0:T(4,128)(2,1)} %query_hbm.1, bf16[3,1024]{1,0:T(4,128)(2,1)} %rope_hbm.1), custom_call_target="tpu_custom_call" | custom-call | flops 4000000000 | bytes 67108864 | tf_op jit(solution)/shard_map/pallas_call | solution.py:133
  5.4 5.1 %all-to-all-start = ((bf16[16,7,8,128]{3,2,1,0:T(8,128)(2,1)}), bf16[16,7,8,128]{3,2,1,0:T(8,128)(2,1)S(1)}, u32[]{:S(2)}, u32[]{:S(2)}) async-start(bf16[16,7,8,128]{3,2,1,0:T(8,128)(2,1)} %shard_map.158), calls=%async_computation | async-start | bytes 458752 | tf_op jit(solution)/shard_map/all_to_all | solution.py:481
  10.5 0.0 copy-done.5
  10.5 0.0 copy-start.4
  10.5 0.5 collective-permute-start.3
  11.0 1.6 %collective-permute-start.1 = (bf16[64,512]{1,0:T(8,128)(2,1)S(1)}, bf16[64,512]{1,0:T(8,128)(2,1)S(1)}, u32[]{:S(2)}, u32[]{:S(2)}) collective-permute-start(bf16[64,512]{1,0:T(8,128)(2,1)S(1)} %copy-done.5), channel_id=1, source_target_pairs={{0,2},{1,5},{2,0},{3,7},{4,6},{5,1},{6,4},{7,3},{8,10},{9,13},{10,... | collective-permute-start | bytes 196616 | tf_op jit(solution)/shard_map/ppermute | solution.py:457
  12.6 0.0 copy-done.10
  12.6 0.6 shard_map.159
  13.3 0.0 collective-permute-done.3.core_rope_ref
  13.3 2.5 %collective-permute-done.1.near_rope_ref = bf16[64,512]{1,0:T(8,128)(2,1)S(1)} collective-permute-done((bf16[64,512]{1,0:T(8,128)(2,1)S(1)}, bf16[64,512]{1,0:T(8,128)(2,1)S(1)}, u32[]{:S(2)}, u32[]{:S(2)}) %collective-permute-start.1) | collective-permute-done | bytes 65568 | tf_op jit(solution)/shard_map/ppermute | solution.py:457
  15.8 4.7 %all-to-all-done.arrived_ref = bf16[16,7,8,128]{3,2,1,0:T(8,128)(2,1)S(1)} async-done(((bf16[16,7,8,128]{3,2,1,0:T(8,128)(2,1)}), bf16[16,7,8,128]{3,2,1,0:T(8,128)(2,1)S(1)}, u32[]{:S(2)}, u32[]{:S(2)}) %all-to-all-start) | async-done | bytes 229408 | tf_op jit(solution)/shard_map/all_to_all | solution.py:481
  20.5 0.0 collective-permute-done.near_ref
  20.5 0.0 collective-permute-done.2.core_ref
  20.5 0.0 collective-permute-start.4
  20.6 0.5 collective-permute-start.5
  21.1 0.0 copy-done.4
  21.1 2.2 %shard_map.160 = (bf16[192,512]{1,0:T(8,128)(2,1)S(1)}, bf16[192,256]{1,0:T(8,128)(2,1)S(1)}, f32[2,192,128]{2,1,0:T(8,128)S(1)}, f32[192,512]{1,0:T(8,128)S(1)}) custom-call(bf16[16,7,8,128]{3,2,1,0:T(8,128)(2,1)S(1)} %all-to-all-done.arrived_ref, bf16[384,384]{1,0:T(8,128)(2,1)S(1)} %get-tuple-element.32.order_ref, ...), custom_call_target="tpu_custom_call" | custom-call | flops 4000000000 | bytes 67108864 | tf_op jit(solution)/shard_map/pallas_call | solution.py:133
  23.3 0.0 collective-permute-done.5.far_rope_ref
  23.3 0.0 collective-permute-done.4.far_ref
  23.3 0.0 copy-start.3
  23.3 0.8 %shard_map.161 = bf16[4,56,512]{2,1,0:T(8,128)(2,1)S(1)} custom-call(bf16[192,512]{1,0:T(8,128)(2,1)S(1)} %get-tuple-element.39.query_ref, bf16[192,256]{1,0:T(8,128)(2,1)S(1)} %get-tuple-element.40.rope_query_ref, f32[2,192,128]{2,1,0:T(8,128)S(1)} %get-tuple-element.41.state_ref, f32[192,512]{1,0:T(8,128)S(1)} %get-tuple-element.42.total_ref, ...), custom_call_target="tpu_custom_call" | custom-call | flops 4000000000 | bytes 67108864 | tf_op jit(solution)/shard_map/pallas_call | solution.py:133
  24.1 11.1 %all_to_all.25.arrived_ref = bf16[4,56,512]{2,1,0:T(8,128)(2,1)S(1)} all-to-all(bf16[4,56,512]{2,1,0:T(8,128)(2,1)S(1)} %shard_map.161), channel_id=1, replica_groups={{0,6,8,14},{1,7,9,15},{2,4,10,12},{3,5,11,13},{16,22,24,30},{17,23,25,3..., dimensions={0} | all-to-all | bytes 458752 | tf_op jit(solution)/shard_map/all_to_all | solution.py:540
  35.2 0.0 copy-done.3
  35.2 0.7 shard_map.162
  35.9 0.1 collective-permute-start.6
  36.0 1.3 %collective-permute-done.6.other_ref = bf16[24,2560]{1,0:T(8,128)(2,1)S(1)} collective-permute-done((bf16[24,2560]{1,0:T(8,128)(2,1)S(1)}, bf16[24,2560]{1,0:T(8,128)(2,1)S(1)}, u32[]{:S(2)}, u32[]{:S(2)}) %collective-permute-start.6) | collective-permute-done | bytes 122912 | tf_op jit(solution)/shard_map/ppermute | solution.py:454
  37.3 0.0 copy-done.11
  37.3 0.2 shard_map.163
  37.5 10.1 %all_to_all.26.arrived_ref = bf16[8,16,512]{2,1,0:T(8,128)(2,1)S(1)} all-to-all(bf16[8,16,512]{2,1,0:T(8,128)(2,1)S(1)} %shard_map.163), channel_id=1, replica_groups={{0,2,4,6,8,10,12,14},{1,3,5,7,9,11,13,15},{16,18,20,22,24,26,28,30},{17..., dimensions={0} | all-to-all | bytes 262144 | tf_op jit(solution)/shard_map/all_to_all | solution.py:540
  47.7 0.0 copy-start.2
  47.7 0.0 copy-start.8
  47.7 0.0 copy-start.9
  47.7 0.0 copy-start.12
  47.7 0.2 shard_map.164
  47.9 10.3 %all_to_all.27.own_rows_ref = bf16[8,16,512]{2,1,0:T(8,128)(2,1)S(1)} all-to-all(bf16[8,16,512]{2,1,0:T(8,128)(2,1)S(1)} %get-tuple-element.45), channel_id=1, replica_groups={{0,2,4,6,8,10,12,14},{1,3,5,7,9,11,13,15},{16,18,20,22,24,26,28,30},{17..., dimensions={0} | all-to-all | bytes 262144 | tf_op jit(solution)/shard_map/all_to_all | solution.py:540
  58.2 0.0 collective-permute-start.7
  58.2 1.3 %collective-permute-done.7.other_rows_ref = bf16[8,16,512]{2,1,0:T(8,128)(2,1)S(1)} collective-permute-done((bf16[8,16,512]{2,1,0:T(8,128)(2,1)S(1)}, bf16[8,16,512]{2,1,0:T(8,128)(2,1)S(1)}, u32[]{:S(2)}, u32[]{:S(2)}) %collective-permute-start.7) | collective-permute-done | bytes 131104 | tf_op jit(solution)/shard_map/ppermute | solution.py:454
  59.5 0.0 copy-done
  59.5 2.3 %shard_map.165 = (f32[24,2560]{1,0:T(8,128)S(1)}, bf16[24,2560]{1,0:T(8,128)(2,1)S(1)}) custom-call(bf16[8,16,512]{2,1,0:T(8,128)(2,1)S(1)} %all_to_all.27.own_rows_ref, bf16[8,16,512]{2,1,0:T(8,128)(2,1)S(1)} %collective-permute-done.7.other_rows_ref, bf16[120,128]{1,0:T(8,128)(2,1)S(1)} %copy-done.12, s32[6,48]{1,0:T(8,128)S(1)} %bitcast.8, ...), custom_call_target="tpu_custom_call" | custom-call | flops 4000000000 | bytes 67108864 | tf_op jit(solution)/shard_map/pallas_call | solution.py:133
  61.9 0.2 collective-permute-start.8
  62.1 1.2 %collective-permute-done.8.other_ref = bf16[24,2560]{1,0:T(8,128)(2,1)S(1)} collective-permute-done((bf16[24,2560]{1,0:T(8,128)(2,1)S(1)}, bf16[24,2560]{1,0:T(8,128)(2,1)S(1)}, u32[]{:S(2)}, u32[]{:S(2)}) %collective-permute-start.8) | collective-permute-done | bytes 122912 | tf_op jit(solution)/shard_map/ppermute | solution.py:454
  63.3 0.2 shard_map.166
  63.5 10.0 %all_to_all.28.arrived_ref = bf16[8,16,512]{2,1,0:T(8,128)(2,1)S(1)} all-to-all(bf16[8,16,512]{2,1,0:T(8,128)(2,1)S(1)} %shard_map.166), channel_id=1, replica_groups={{0,2,4,6,8,10,12,14},{1,3,5,7,9,11,13,15},{16,18,20,22,24,26,28,30},{17..., dimensions={0} | all-to-all | bytes 262144 | tf_op jit(solution)/shard_map/all_to_all | solution.py:540
  73.4 0.7 shard_map.167
  (12 shorter events, 0.0 us)
Async XLA Ops:
  0.6 9.9 %copy-start.5 = (bf16[64,512]{1,0:T(8,128)(2,1)S(1)}, bf16[64,512]{1,0:T(8,128)(2,1)}, u32[]{:S(2)}) copy-start(bf16[64,512]{1,0:T(8,128)(2,1)} %own_rope_ref.1) | copy-start | bytes 196612
  0.6 12.0 %copy-start.10 = (s32[48]{0:T(128)S(1)}, s32[48]{0:T(128)}, u32[]{:S(2)}) copy-start(s32[48]{0:T(128)} %length_ref.1) | copy-start | bytes 580
  0.7 19.9 %collective-permute-start = (bf16[512,512]{1,0:T(8,128)(2,1)}, bf16[512,512]{1,0:T(8,128)(2,1)S(1)}, u32[]{:S(2)}, u32[]{:S(2)}) collective-permute-start(bf16[512,512]{1,0:T(8,128)(2,1)} %own_ref.1), channel_id=1, source_target_pairs={{0,2},{1,5},{2,0},{3,7},{4,6},{5,1},{6,4},{7,3},{8,10},{9,13},{10,... | collective-permute-start | bytes 1572872 | tf_op jit(solution)/shard_map/ppermute | solution.py:457
  3.7 16.8 %collective-permute-start.2 = (bf16[512,512]{1,0:T(8,128)(2,1)}, bf16[512,512]{1,0:T(8,128)(2,1)S(1)}, u32[]{:S(2)}, u32[]{:S(2)}) collective-permute-start(bf16[512,512]{1,0:T(8,128)(2,1)} %own_ref.1), channel_id=1, source_target_pairs={{0,1},{1,0},{2,3},{3,2},{4,5},{5,4},{6,7},{7,6},{8,9},{9,8},{10,11... | collective-permute-start | bytes 1572872 | tf_op jit(solution)/shard_map/ppermute | solution.py:454
  5.4 15.2 %all-to-all-start = ((bf16[16,7,8,128]{3,2,1,0:T(8,128)(2,1)}), bf16[16,7,8,128]{3,2,1,0:T(8,128)(2,1)S(1)}, u32[]{:S(2)}, u32[]{:S(2)}) async-start(bf16[16,7,8,128]{3,2,1,0:T(8,128)(2,1)} %shard_map.158), calls=%async_computation | async-start | bytes 458752 | tf_op jit(solution)/shard_map/all_to_all | solution.py:481
  10.5 10.6 %copy-start.4 = (bf16[512,512]{1,0:T(8,128)(2,1)S(1)}, bf16[512,512]{1,0:T(8,128)(2,1)}, u32[]{:S(2)}) copy-start(bf16[512,512]{1,0:T(8,128)(2,1)} %own_ref.1) | copy-start | bytes 1572868
  10.5 2.8 %collective-permute-start.3 = (bf16[64,512]{1,0:T(8,128)(2,1)S(1)}, bf16[64,512]{1,0:T(8,128)(2,1)S(1)}, u32[]{:S(2)}, u32[]{:S(2)}) collective-permute-start(bf16[64,512]{1,0:T(8,128)(2,1)S(1)} %copy-done.5), channel_id=1, source_target_pairs={{0,1},{1,0},{2,3},{3,2},{4,5},{5,4},{6,7},{7,6},{8,9},{9,8},{10,11... | collective-permute-start | bytes 196616 | tf_op jit(solution)/shard_map/ppermute | solution.py:454
  11.0 4.8 %collective-permute-start.1 = (bf16[64,512]{1,0:T(8,128)(2,1)S(1)}, bf16[64,512]{1,0:T(8,128)(2,1)S(1)}, u32[]{:S(2)}, u32[]{:S(2)}) collective-permute-start(bf16[64,512]{1,0:T(8,128)(2,1)S(1)} %copy-done.5), channel_id=1, source_target_pairs={{0,2},{1,5},{2,0},{3,7},{4,6},{5,1},{6,4},{7,3},{8,10},{9,13},{10,... | collective-permute-start | bytes 196616 | tf_op jit(solution)/shard_map/ppermute | solution.py:457
  20.5 2.7 %collective-permute-start.4 = (bf16[512,512]{1,0:T(8,128)(2,1)S(1)}, bf16[512,512]{1,0:T(8,128)(2,1)S(1)}, u32[]{:S(2)}, u32[]{:S(2)}) collective-permute-start(bf16[512,512]{1,0:T(8,128)(2,1)S(1)} %collective-permute-done.near_ref), channel_id=1, source_target_pairs={{0,1},{1,0},{2,3},{3,2},{4,5},{5,4},{6,7},{7,6},{8,9},{9,8},{10,11... | collective-permute-start | bytes 1572872 | tf_op jit(solution)/shard_map/ppermute | solution.py:454
  20.6 2.7 %collective-permute-start.5 = (bf16[64,512]{1,0:T(8,128)(2,1)S(1)}, bf16[64,512]{1,0:T(8,128)(2,1)S(1)}, u32[]{:S(2)}, u32[]{:S(2)}) collective-permute-start(bf16[64,512]{1,0:T(8,128)(2,1)S(1)} %collective-permute-done.1.near_rope_ref), channel_id=1, source_target_pairs={{0,1},{1,0},{2,3},{3,2},{4,5},{5,4},{6,7},{7,6},{8,9},{9,8},{10,11... | collective-permute-start | bytes 196616 | tf_op jit(solution)/shard_map/ppermute | solution.py:454
  23.3 11.9 %copy-start.3 = (bf16[512,2560]{1,0:T(8,128)(2,1)S(1)}, bf16[512,2560]{1,0:T(8,128)(2,1)}, u32[]{:S(2)}) copy-start(bf16[512,2560]{1,0:T(8,128)(2,1)} %weight_ref.1) | copy-start | bytes 7864324
  35.2 2.1 %copy-start.11 = (bf16[128,120]{1,0:T(8,128)(2,1)S(1)}, bf16[128,120]{1,0:T(8,128)(2,1)}, u32[]{:S(2)}) copy-start(bf16[128,120]{1,0:T(8,128)(2,1)} %constant.4.clone.order_ref) | copy-start | bytes 92164
  35.9 1.4 %collective-permute-start.6 = (bf16[24,2560]{1,0:T(8,128)(2,1)S(1)}, bf16[24,2560]{1,0:T(8,128)(2,1)S(1)}, u32[]{:S(2)}, u32[]{:S(2)}) collective-permute-start(bf16[24,2560]{1,0:T(8,128)(2,1)S(1)} %get-tuple-element.44), channel_id=1, source_target_pairs={{0,1},{1,0},{2,3},{3,2},{4,5},{5,4},{6,7},{7,6},{8,9},{9,8},{10,11... | collective-permute-start | bytes 368648 | tf_op jit(solution)/shard_map/ppermute | solution.py:454
  37.3 10.3 %copy-start.6 = (bf16[3,2560]{1,0:T(4,128)(2,1)S(1)}, bf16[3,2560]{1,0:T(4,128)(2,1)}, u32[]{:S(2)}) copy-start(bf16[3,2560]{1,0:T(4,128)(2,1)} %residual_ref.1) | copy-start | bytes 46084
  37.3 10.3 %copy-start.7 = (f32[2560]{0:T(1024)S(1)}, f32[2560]{0:T(1024)}, u32[]{:S(2)}) copy-start(f32[2560]{0:T(1024)} %gain_ref.1) | copy-start | bytes 30724
  47.7 11.8 %copy-start = (bf16[1,2560,768]{2,1,0:T(8,128)(2,1)S(1)}, bf16[1,2560,768]{2,1,0:T(8,128)(2,1)}, u32[]{:S(2)}) copy-start(bf16[1,2560,768]{2,1,0:T(8,128)(2,1)} %param.25) | copy-start | bytes 11796484
  47.7 11.8 %copy-start.1 = (bf16[1,2560,768]{2,1,0:T(8,128)(2,1)S(1)}, bf16[1,2560,768]{2,1,0:T(8,128)(2,1)}, u32[]{:S(2)}) copy-start(bf16[1,2560,768]{2,1,0:T(8,128)(2,1)} %param.26) | copy-start | bytes 11796484
  47.7 11.8 %copy-start.2 = (bf16[1,768,2560]{2,1,0:T(8,128)(2,1)S(1)}, bf16[1,768,2560]{2,1,0:T(8,128)(2,1)}, u32[]{:S(2)}) copy-start(bf16[1,768,2560]{2,1,0:T(8,128)(2,1)} %param.27) | copy-start | bytes 11796484
  47.7 11.8 %copy-start.8 = (s32[48,6]{0,1:T(8,128)S(1)}, s32[48,6]{0,1:T(8,128)}, u32[]{:S(2)}) copy-start(s32[48,6]{0,1:T(8,128)} %param.23) | copy-start | bytes 3460
  47.7 11.8 %copy-start.9 = (f32[48,6]{0,1:T(8,128)S(1)}, f32[48,6]{0,1:T(8,128)}, u32[]{:S(2)}) copy-start(f32[48,6]{0,1:T(8,128)} %param.24) | copy-start | bytes 3460
  47.7 11.8 %copy-start.12 = (bf16[120,128]{1,0:T(8,128)(2,1)S(1)}, bf16[120,128]{1,0:T(8,128)(2,1)}, u32[]{:S(2)}) copy-start(bf16[120,128]{1,0:T(8,128)(2,1)} %constant.5.clone.back_ref) | copy-start | bytes 92164
  58.2 1.3 %collective-permute-start.7 = (bf16[8,16,512]{2,1,0:T(8,128)(2,1)S(1)}, bf16[8,16,512]{2,1,0:T(8,128)(2,1)S(1)}, u32[]{:S(2)}, u32[]{:S(2)}) collective-permute-start(bf16[8,16,512]{2,1,0:T(8,128)(2,1)S(1)} %all_to_all.27.own_rows_ref), channel_id=1, source_target_pairs={{0,1},{1,0},{2,3},{3,2},{4,5},{5,4},{6,7},{7,6},{8,9},{9,8},{10,11... | collective-permute-start | bytes 393224 | tf_op jit(solution)/shard_map/ppermute | solution.py:454
  61.9 1.4 %collective-permute-start.8 = (bf16[24,2560]{1,0:T(8,128)(2,1)S(1)}, bf16[24,2560]{1,0:T(8,128)(2,1)S(1)}, u32[]{:S(2)}, u32[]{:S(2)}) collective-permute-start(bf16[24,2560]{1,0:T(8,128)(2,1)S(1)} %get-tuple-element.47), channel_id=1, source_target_pairs={{0,1},{1,0},{2,3},{3,2},{4,5},{5,4},{6,7},{7,6},{8,9},{9,8},{10,11... | collective-permute-start | bytes 368648 | tf_op jit(solution)/shard_map/ppermute | solution.py:454
